TPU v7x, 32 devices: a whole 2x2x4 slice. The times are simulated.
32 devices in a mesh: freq: 16 (over z, y, core), chan: 2 (over x).
Axes of the slice: x: 2, y: 2, z: 4, core: 2. Of those that a mesh axis runs over, the one named last changes fastest.
Arguments:
- traces: bfloat16 [256, 2048, 256], P('freq', 'chan'), may hold values from -6 to 6
- channel_mask: int32 [2048], P('chan'), may hold values 0 or 1
- bin_index: int32 [16], replicated, may hold values from 1 to 127
Outputs:
- cross: bfloat16 [16, 2, 2048, 2048], P('freq', None, 'chan')
All inputs are finite; a program needn't handle non-finite values. No bound on the sum of `channel_mask` on one device may be relied on, other than what follows from the above.
Results may differ from a plain program's by a relative error of at most 0.0064.
Values may be sent and summed in bfloat16 or wider, within the bound.
No kernel may reach another device: no remote copies, remote signals or barrier semaphores. Data moves between devices by JAX's collectives and lax.ppermute only.
A program may use at most 64 MiB of HBM per device.

v0:
```python
import math
import jax
import jax.numpy as jnp
from jax import lax
from jax.sharding import PartitionSpec as P


def passed_along(value, axis, steps):
    count = lax.axis_size(axis)
    pairs = [(source, (source + steps) % count) for source in range(count)]
    return lax.ppermute(value, axis, pairs)


def shards(traces, channel_mask, bin_index):
    segment_local_rows, width, length = traces.shape
    nbins = bin_index.shape[0]
    samples = jnp.arange(length, dtype=jnp.int32)
    phase_index = bin_index[None, :] * samples[:, None] % length
    angles = 2.0 * math.pi / length * phase_index.astype(jnp.float32)
    wave_table = (
        jnp.stack([jnp.cos(angles), -jnp.sin(angles)], axis=2)
        .reshape(length, 2 * nbins)
        .astype(jnp.bfloat16)
    )
    taper_curve = 0.5 - 0.5 * jnp.cos(2.0 * math.pi / length * (samples.astype(jnp.float32) + 0.5))
    channel_gain = channel_mask.astype(jnp.float32)
    squares = jnp.einsum("sct,sct->sc", traces, traces, preferred_element_type=jnp.float32)
    spread = jnp.sqrt(squares / length + 1e-06)
    tapered = (
        traces.astype(jnp.float32)
        / spread[:, :, None]
        * taper_curve[None, None, :]
        * channel_gain[None, :, None]
    ).astype(jnp.bfloat16)
    segment_spectra = jnp.dot(
        tapered.reshape(segment_local_rows * width, length),
        wave_table,
        preferred_element_type=jnp.float32,
    )
    segment_spectra = segment_spectra.reshape(segment_local_rows, width, nbins, 2).transpose(
        2, 0, 3, 1
    )
    segment_spectra = lax.all_to_all(
        segment_spectra, "freq", split_axis=0, concat_axis=1, tiled=True
    )
    bins_local = segment_spectra.shape[0]
    segments = segment_spectra.shape[1]
    band_power = jnp.sum(segment_spectra * segment_spectra, axis=(1, 2)) / segments + 1e-06
    whitened = (segment_spectra / jnp.sqrt(band_power)[:, None, None, :]).astype(jnp.bfloat16)
    real_rows = whitened.reshape(bins_local, 2 * segments, width)
    turned = jnp.stack([whitened[:, :, 1], -whitened[:, :, 0]], axis=2).reshape(
        bins_local, 2 * segments, width
    )
    stacked_spectra = jnp.concatenate([real_rows, turned], axis=2)
    inverse = 1.0 / segments

    def block_cross_product(spectrum_fragment):
        cross_product_term = jnp.einsum(
            "mqr,mqe->mre", stacked_spectra, spectrum_fragment, preferred_element_type=jnp.float32
        )
        return (
            (cross_product_term * inverse)
            .reshape(bins_local, 2, width, spectrum_fragment.shape[2])
            .astype(jnp.bfloat16)
        )

    def place(result, spectrum_fragment, column):
        return lax.dynamic_update_slice(
            result, block_cross_product(spectrum_fragment), (0, 0, 0, column)
        )

    group = lax.axis_size("chan")
    own_index = lax.axis_index("chan")
    result = jnp.zeros((bins_local, 2, width, group * width), jnp.bfloat16)
    result = place(result, real_rows, own_index * width)
    moving = real_rows
    for step in range(1, group):
        moving = passed_along(moving, "chan", 1)
        result = place(result, moving, (own_index - step) % group * width)
    return result


def solution(mesh):
    in_specs = (P("freq", "chan", None), P("chan"), P())
    out_specs = P("freq", None, "chan", None)
    return jax.shard_map(shards, mesh=mesh, in_specs=in_specs, out_specs=out_specs, check_vma=False)
```

profile of v0, /device:TPU:14, one launch (start us, length us, event | category | flops | bytes accessed | tf_op | source)
XLA Modules:
  0.0 106.8 jit_solution(10640829522992178758)
XLA Ops:
  0.0 0.8 cosine_convert_fusion
  0.9 0.0 copy-start.3
  0.9 0.0 copy-start
  1.0 5.8 %fusion.3 = f32[16,1024]{1,0:T(8,128)S(1)} fusion(bf16[16,1024,256]{2,1,0:T(8,128)(2,1)} %param.3), kind=kLoop, calls=%fused_computation.5 | loop fusion | flops 12566528 | bytes 8454144 | tf_op jit(solution)/shard_map/sct,sct->sc/dot_general | solution.py:27
  6.8 0.0 copy-done.3
  6.8 0.0 copy-done
  6.8 3.3 %fusion.8 = f32[16,16,2,1024]{3,0,2,1:T(8,128)S(1)} fusion(bf16[16,1024,256]{2,1,0:T(8,128)(2,1)S(1)} %copy-done, f32[1024]{0:T(1024)S(1)} %convert_element_type.90, f32[256]{0:T(256)S(1)} %multiply_subtract_fusion, f32[16,1024]{1,0:T(8,128)S(1)} %add_sqrt_fusion, bf16[16,2,256]{2,1,0:T(2,128)(2,1)S(1)} %dot_general.18), kind=kOutput, calls=%fused_computation.16 | convolution fusion | flops 289406976 | bytes 10572800 | tf_op jit(solution)/shard_map/dot_general | solution.py:35
  10.1 2.9 %copy.15 = f32[16,16,2,1024]{3,2,1,0:T(2,128)} copy(f32[16,16,2,1024]{3,0,2,1:T(8,128)S(1)} %fusion.8) | data formatting | bytes 4194304 | tf_op jit(solution)/shard_map/transpose | solution.py:40
  13.0 6.2 %all-to-all-start = ((f32[16,16,2,1024]{3,2,1,0:T(2,128)}), f32[16,16,2,1024]{3,2,1,0:T(2,128)S(1)}, u32[]{:S(2)}, u32[]{:S(2)}) async-start(f32[16,16,2,1024]{3,2,1,0:T(2,128)} %copy.15), calls=%async_computation | async-start | bytes 4194304 | tf_op jit(solution)/shard_map/all_to_all | solution.py:43
  19.3 47.1 %all-to-all-done = f32[16,16,2,1024]{3,2,1,0:T(2,128)S(1)} async-done(((f32[16,16,2,1024]{3,2,1,0:T(2,128)}), f32[16,16,2,1024]{3,2,1,0:T(2,128)S(1)}, u32[]{:S(2)}, u32[]{:S(2)}) %all-to-all-start) | async-done | bytes 2097184 | tf_op jit(solution)/shard_map/all_to_all | solution.py:43
  66.4 0.9 multiply_reduce_fusion
  67.3 0.7 copy.16
  68.0 1.2 %fusion.7 = bf16[1,256,2,1024]{3,1,2,0:T(8,128)(2,1)} fusion(f32[16,16,2,1024]{3,1,0,2:T(8,128)S(1)} %copy.16, f32[1024]{0:T(1024)S(1)} %add_sqrt_fusion.1), kind=kLoop, calls=%fused_computation.12 | loop fusion | flops 1048576 | bytes 3149824 | tf_op jit(solution)/shard_map/convert_element_type | solution.py:49
  69.2 2.4 %all_to_all.12 = f32[1,512,1024]{2,1,0:T(8,128)} reshape(f32[16,16,2,1024]{3,2,1,0:T(2,128)S(1)} %all-to-all-done) | data formatting | bytes 4194304 | tf_op jit(solution)/shard_map/all_to_all | solution.py:43
  71.7 0.0 copy-start.2
  71.7 2.9 %divide_convert_fusion = bf16[1,512,1024]{2,1,0:T(8,128)(2,1)} fusion(f32[1,512,1024]{2,1,0:T(8,128)} %all_to_all.12, f32[1024]{0:T(1024)S(1)} %add_sqrt_fusion.1), kind=kLoop, calls=%fused_computation.13 | loop fusion | flops 1048576 | bytes 3149824 | tf_op jit(solution)/shard_map/convert_element_type | solution.py:49
  74.6 0.5 collective-permute-start
  75.1 0.9 divide_convert_fusion.1
  76.0 0.0 copy-done.2
  76.0 0.1 fusion.22
  76.1 0.1 pad_maximum_fusion
  76.2 1.1 %copy.17 = bf16[1,256,2,1024]{3,2,1,0:T(2,128)(2,1)S(1)} copy(bf16[1,256,2,1024]{3,1,2,0:T(8,128)(2,1)S(1)} %pad_maximum_fusion) | data formatting | bytes 2097152 | tf_op jit(solution)/shard_map/stack | solution.py:51
  77.3 0.4 reshape.233
  77.7 0.4 convert_element_type.97
  78.2 3.6 %multiply_convert_fusion.1 = bf16[2048,1024]{1,0:T(8,128)(2,1)S(1)} fusion(bf16[512,1024]{1,0:T(8,128)(2,1)S(1)} %convert_element_type.97, bf16[1,512,1024]{2,1,0:T(8,128)(2,1)S(1)} %reshape.233, bf16[1,512,1024]{2,1,0:T(8,128)(2,1)} %divide_convert_fusion), kind=kOutput, calls=%fused_computation.8 | convolution fusion | flops 2155872256 | bytes 7340032 | tf_op jit(solution)/shard_map/mqr,mqe->mre/dot_general | solution.py:58
  81.8 1.1 broadcast_in_dim.2
  82.9 0.6 constant_dynamic-update-slice_fusion.1
  83.5 0.0 copy-start.1
  83.5 16.9 %collective-permute-done = bf16[1,512,1024]{2,1,0:T(8,128)(2,1)} collective-permute-done((bf16[1,512,1024]{2,1,0:T(8,128)(2,1)}, bf16[1,512,1024]{2,1,0:T(8,128)(2,1)}, u32[]{:S(2)}, u32[]{:S(2)}) %collective-permute-start) | collective-permute-done | bytes 1048608 | tf_op jit(solution)/shard_map/ppermute | solution.py:11
  100.4 3.9 %multiply_convert_fusion = bf16[2048,1024]{1,0:T(8,128)(2,1)S(1)} fusion(bf16[1,512,1024]{2,1,0:T(8,128)(2,1)S(1)} %reshape.233, bf16[1,512,1024]{2,1,0:T(8,128)(2,1)} %divide_convert_fusion, bf16[1,512,1024]{2,1,0:T(8,128)(2,1)} %collective-permute-done), kind=kOutput, calls=%fused_computation.7 | convolution fusion | flops 2155872256 | bytes 7340032 | tf_op jit(solution)/shard_map/mqr,mqe->mre/dot_general | solution.py:58
  104.3 0.0 copy-done.1
  104.3 2.5 %constant_dynamic-update-slice_fusion = bf16[1,2,1024,2048]{3,2,1,0:T(8,128)(2,1)} fusion(bf16[1,2,1024,2048]{3,2,1,0:T(8,128)(2,1)} %copy-done.1, bf16[1,2,1024,1024]{3,2,1,0:T(8,128)(2,1)S(1)} %bitcast.29, s32[]{:T(128)S(6)} %select_n.33), kind=kLoop, calls=%fused_computation.37 | loop fusion | bytes 8388612 | tf_op jit(solution)/shard_map/dynamic_update_slice | solution.py:68
  (8 shorter events, 0.1 us)
Async XLA Ops:
  0.9 5.8 %copy-start.3 = (s32[1024]{0:T(1024)S(1)}, s32[1024]{0:T(1024)}, u32[]{:S(2)}) copy-start(s32[1024]{0:T(1024)} %param.4) | copy-start | bytes 12292
  0.9 5.8 %copy-start = (bf16[16,1024,256]{2,1,0:T(8,128)(2,1)S(1)}, bf16[16,1024,256]{2,1,0:T(8,128)(2,1)}, u32[]{:S(2)}) copy-start(bf16[16,1024,256]{2,1,0:T(8,128)(2,1)} %param.3) | copy-start | bytes 25165828
  13.0 53.4 %all-to-all-start = ((f32[16,16,2,1024]{3,2,1,0:T(2,128)}), f32[16,16,2,1024]{3,2,1,0:T(2,128)S(1)}, u32[]{:S(2)}, u32[]{:S(2)}) async-start(f32[16,16,2,1024]{3,2,1,0:T(2,128)} %copy.15), calls=%async_computation | async-start | bytes 4194304 | tf_op jit(solution)/shard_map/all_to_all | solution.py:43
  71.7 4.4 %copy-start.2 = (bf16[1,256,2,1024]{3,1,2,0:T(8,128)(2,1)S(1)}, bf16[1,256,2,1024]{3,1,2,0:T(8,128)(2,1)}, u32[]{:S(2)}) copy-start(bf16[1,256,2,1024]{3,1,2,0:T(8,128)(2,1)} %fusion.7) | copy-start | bytes 3145732
  74.6 25.8 %collective-permute-start = (bf16[1,512,1024]{2,1,0:T(8,128)(2,1)}, bf16[1,512,1024]{2,1,0:T(8,128)(2,1)}, u32[]{:S(2)}, u32[]{:S(2)}) collective-permute-start(bf16[1,512,1024]{2,1,0:T(8,128)(2,1)} %divide_convert_fusion), channel_id=1, source_target_pairs={{0,1},{1,0},{2,3},{3,2},{4,5},{5,4},{6,7},{7,6},{8,9},{9,8},{10,11... | collective-permute-start | bytes 3145736 | tf_op jit(solution)/shard_map/ppermute | solution.py:11
  83.5 20.8 %copy-start.1 = (bf16[1,2,1024,2048]{3,2,1,0:T(8,128)(2,1)}, bf16[1,2,1024,2048]{3,2,1,0:T(8,128)(2,1)S(1)}, u32[]{:S(2)}) copy-start(bf16[1,2,1024,2048]{3,2,1,0:T(8,128)(2,1)S(1)} %constant_dynamic-update-slice_fusion.1) | copy-start | bytes 25165828
where the time goes:
time: 107 us
  waiting for transfers between devices  64 us (60%)
  other arithmetic  12.8 us (12%)
  local copies, waits for them, and re-layouts  12.2 us (11%)
  matrix products  10.8 us (10%)
  starting transfers between devices  6.78 us (6%)
    all_to_all x1, waiting for transfers between devices, shards(): lax.all_to_all(segment_spectra, 'freq', split_axis=0, concat_axis=1, tile...  47.1 us
    ppermute x1, waiting for transfers between devices, passed_along(): return lax.ppermute(value, axis, pairs)  16.9 us
    dot_general x2, matrix products, block_cross_product(): jnp.einsum('mqr,mqe->mre', stacked_spectra, spectrum_fragment, preferred_...  7.53 us
    all_to_all x1, starting transfers between devices, shards(): lax.all_to_all(segment_spectra, 'freq', split_axis=0, concat_axis=1, tile...  6.24 us
    dot_general x1, other arithmetic, shards(): jnp.einsum('sct,sct->sc', traces, traces, preferred_element_type=jnp.floa...  5.77 us
    convert_element_type x3, other arithmetic, shards(): (segment_spectra / jnp.sqrt(band_power)[:, None, None, :]).astype(jnp.bfl...  5.04 us
    dot_general x1, matrix products, shards(): jnp.dot(tapered.reshape(segment_local_rows * width, length), wave_table,...  3.3 us
    all_to_all x2, local copies, waits for them, and re-layouts, shards(): lax.all_to_all(segment_spectra, 'freq', split_axis=0, concat_axis=1, tile...  3.09 us
  transfers between devices with their start and end apart: 2, of which 2 were waited for; matrix products, arithmetic and copies ran while one was open for 8% of the time, Pallas kernels for 0%

commit v1 on v0

--- a/solution.py
+++ b/solution.py
@@ -40,8 +40,11 @@
     segment_spectra = segment_spectra.reshape(segment_local_rows, width, nbins, 2).transpose(
         2, 0, 3, 1
     )
-    segment_spectra = lax.all_to_all(
-        segment_spectra, "freq", split_axis=0, concat_axis=1, tiled=True
+    segment_spectra = jnp.concatenate(
+        lax.all_to_all(
+            jnp.stack(jnp.split(segment_spectra, lax.axis_size("freq"), axis=0)), "freq", 0, 0
+        ),
+        axis=1,
     )
     bins_local = segment_spectra.shape[0]
     segments = segment_spectra.shape[1]

time: 107 us -> 134 us (1.25)
  local copies, waits for them, and re-layouts: 12.2 us -> 27.1 us
  other arithmetic: 12.8 us -> 22.5 us
  matrix products: 10.8 us -> 14.3 us
    another operation x0 -> x3, local copies, waits for them, and re-layouts: none -> 9.91 us  [shards(): jnp.stack(jnp.split(segment_spectra, lax.axis_size('freq'), axis=0))]
    concatenate x0 -> x1, other arithmetic: none -> 8.59 us  [shards(): stacked_spectra = jnp.concatenate([real_rows, turned], axis=2)]
    reshape x0 -> x1, local copies, waits for them, and re-layouts: none -> 4.24 us  [shards(): jnp.concatenate(lax.all_to_all(jnp.stack(jnp.split(segment_spectra, lax.a...]
    dot_general x2, matrix products: 7.53 us -> 11 us  [block_cross_product(): jnp.einsum('mqr,mqe->mre', stacked_spectra, spectrum_fragment, preferred_...]
    convert_element_type x1 -> x2, local copies, waits for them, and re-layouts: 0.44 us -> 3.67 us  [shards(): (segment_spectra / jnp.sqrt(band_power)[:, None, None, :]).astype(jnp.bfl...]
    transpose x1 -> x0, local copies, waits for them, and re-layouts: 2.94 us -> none  [shards(): segment_spectra.reshape(segment_local_rows, width, nbins, 2)]
    reshape x1, local copies, waits for them, and re-layouts: 0.44 us -> 3.33 us  [shards(): jnp.stack([whitened[:, :, 1], -whitened[:, :, 0]], axis=2)]
    all_to_all x2 -> x1, local copies, waits for them, and re-layouts: 3.09 us -> 0.68 us  [shards(): lax.all_to_all(jnp.stack(jnp.split(segment_spectra, lax.axis_size('freq')...]
  transfers between devices with their start and end apart: 2 -> 2, of which waited for: 2 -> 2; matrix products, arithmetic and copies ran while one was open for 8% -> 7% of each run, Pallas kernels for 0% -> 0%
where the time goes in v1:
time: 134 us
  waiting for transfers between devices  63.1 us (47%)
  local copies, waits for them, and re-layouts  27.1 us (20%)
  other arithmetic  22.5 us (17%)
  matrix products  14.3 us (11%)
  starting transfers between devices  6.78 us (5%)
    all_to_all x1, waiting for transfers between devices, shards(): lax.all_to_all(jnp.stack(jnp.split(segment_spectra, lax.axis_size('freq')...  47.1 us
    ppermute x1, waiting for transfers between devices, passed_along(): return lax.ppermute(value, axis, pairs)  15.9 us
    dot_general x2, matrix products, block_cross_product(): jnp.einsum('mqr,mqe->mre', stacked_spectra, spectrum_fragment, preferred_...  11 us
    another operation x3, local copies, waits for them, and re-layouts, shards(): jnp.stack(jnp.split(segment_spectra, lax.axis_size('freq'), axis=0))  9.91 us
    concatenate x1, other arithmetic, shards(): stacked_spectra = jnp.concatenate([real_rows, turned], axis=2)  8.59 us
    all_to_all x1, starting transfers between devices, shards(): lax.all_to_all(jnp.stack(jnp.split(segment_spectra, lax.axis_size('freq')...  6.24 us
    dot_general x1, other arithmetic, shards(): jnp.einsum('sct,sct->sc', traces, traces, preferred_element_type=jnp.floa...  5.77 us
    convert_element_type x3, other arithmetic, shards(): (segment_spectra / jnp.sqrt(band_power)[:, None, None, :]).astype(jnp.bfl...  5.46 us
  transfers between devices with their start and end apart: 2, of which 2 were waited for; matrix products, arithmetic and copies ran while one was open for 7% of the time, Pallas kernels for 0%

profile of v1, /device:TPU:14, one launch (start us, length us, event | category | flops | bytes accessed | tf_op | source)
XLA Modules:
  0.0 133.8 jit_solution(11098134617697180132)
XLA Ops:
  0.0 0.7 convert_element_type.90
  0.7 0.8 cosine_convert_fusion
  1.6 0.0 copy-start
  1.6 5.8 %fusion.3 = f32[16,1024]{1,0:T(8,128)S(1)} fusion(bf16[16,1024,256]{2,1,0:T(8,128)(2,1)} %param.3), kind=kLoop, calls=%fused_computation.5 | loop fusion | flops 12566528 | bytes 8454144 | tf_op jit(solution)/shard_map/sct,sct->sc/dot_general | solution.py:27
  7.4 0.0 copy-done
  7.4 3.3 %fusion.10 = f32[16,16,2,1024]{3,0,2,1:T(8,128)S(1)} fusion(bf16[16,1024,256]{2,1,0:T(8,128)(2,1)S(1)} %copy-done, f32[1024]{0:T(1024)S(1)} %convert_element_type.90, f32[256]{0:T(256)S(1)} %multiply_subtract_fusion, f32[16,1024]{1,0:T(8,128)S(1)} %add_sqrt_fusion, bf16[16,2,256]{2,1,0:T(2,128)(2,1)S(1)} %dot_general.18), kind=kOutput, calls=%fused_computation.18 | convolution fusion | flops 289406976 | bytes 10572800 | tf_op jit(solution)/shard_map/dot_general | solution.py:35
  10.7 2.5 %slice_bitcast_fusion = (f32[1,1,16,2,1024]{4,0,3,2,1:T(1,128)S(1)}, f32[1,1,16,2,1024]{4,0,3,2,1:T(1,128)S(1)}, f32[1,1,16,2,1024]{4,0,3,2,1:T(1,128)S(1)}, f32...) fusion(f32[16,16,2,1024]{3,0,2,1:T(8,128)S(1)} %fusion.10), kind=kLoop, calls=%fused_computation.24 | loop fusion | bytes 4194304 | tf_op jit(solution)/shard_map/stack | solution.py:45
  13.3 4.4 %stack.78 = f32[16,1,16,2,1024]{4,0,3,2,1:T(8,128)S(1)} concatenate(f32[1,1,16,2,1024]{4,0,3,2,1:T(1,128)} %get-tuple-element.20, f32[1,1,16,2,1024]{4,0,3,2,1:T(1,128)} %get-tuple-element.19, f32[1,1,16,2,1024]{4,0,3,2,1:T(1,128)} %get-tuple-element.18, f32[1,1,16,2,1024]{4,0,3,2,1:T(1,128)} %get-tuple-element.17, f32[1,1,16,2,1024]{4,0,3,2,1:T(1,128)} %get-tuple-element.16, ...), dimensions={0} | concatenate | bytes 4194304 | tf_op jit(solution)/shard_map/stack | solution.py:45
  17.7 2.9 %copy.23 = f32[16,1,16,2,1024]{4,3,2,1,0:T(2,128)} copy(f32[16,1,16,2,1024]{4,0,3,2,1:T(8,128)S(1)} %stack.78) | data formatting | bytes 4194304 | tf_op jit(solution)/shard_map/stack | solution.py:45
  20.7 6.2 %all-to-all-start = ((f32[16,1,16,2,1024]{4,3,2,1,0:T(2,128)}), f32[16,1,16,2,1024]{4,3,2,1,0:T(2,128)S(1)}, u32[]{:S(2)}, u32[]{:S(2)}) async-start(f32[16,1,16,2,1024]{4,3,2,1,0:T(2,128)} %copy.23), calls=%async_computation | async-start | bytes 4194304 | tf_op jit(solution)/shard_map/all_to_all | solution.py:44
  26.9 47.1 %all-to-all-done = f32[16,1,16,2,1024]{4,3,2,1,0:T(2,128)S(1)} async-done(((f32[16,1,16,2,1024]{4,3,2,1,0:T(2,128)}), f32[16,1,16,2,1024]{4,3,2,1,0:T(2,128)S(1)}, u32[]{:S(2)}, u32[]{:S(2)}) %all-to-all-start) | async-done | bytes 2097184 | tf_op jit(solution)/shard_map/all_to_all | solution.py:44
  74.0 0.9 multiply_reduce_fusion
  74.9 0.7 copy.24
  75.6 0.3 fusion.9
  75.9 4.2 %reshape.235 = f32[1,512,1024]{2,0,1:T(1,128)} reshape(f32[16,1,16,2,1024]{4,3,2,1,0:T(2,128)S(1)} %all-to-all-done) | data formatting | bytes 4194304 | tf_op jit(solution)/shard_map/reshape | solution.py:43
  80.1 4.3 %divide_convert_fusion = bf16[1,512,1024]{2,0,1:T(2,128)(2,1)} fusion(f32[1,512,1024]{2,0,1:T(1,128)} %reshape.235, f32[1024]{0:T(1024)S(1)} %add_sqrt_fusion.1), kind=kLoop, calls=%fused_computation.15 | loop fusion | flops 1048576 | bytes 3149824 | tf_op jit(solution)/shard_map/convert_element_type | solution.py:52
  84.5 0.1 fusion.24
  84.6 0.1 pad_maximum_fusion.1
  84.7 1.1 copy.25
  85.7 3.3 %reshape.244 = bf16[1,512,1024]{2,0,1:T(2,128)(2,1)} reshape(bf16[1,256,2,1024]{3,2,1,0:T(2,128)(2,1)S(1)} %copy.25) | data formatting | bytes 2097152 | tf_op jit(solution)/shard_map/reshape | solution.py:54
  89.1 3.0 %copy.27 = bf16[1,512,1024]{2,1,0:T(8,128)(2,1)} copy(bf16[1,512,1024]{2,0,1:T(2,128)(2,1)} %divide_convert_fusion) | data formatting | bytes 2097152 | tf_op jit(solution)/shard_map/convert_element_type | solution.py:52
  92.0 8.6 %pad_maximum_fusion = bf16[1,512,2048]{2,0,1:T(2,128)(2,1)} fusion(bf16[1,512,1024]{2,0,1:T(2,128)(2,1)} %reshape.244, bf16[1,512,1024]{2,0,1:T(2,128)(2,1)} %divide_convert_fusion), kind=kLoop, calls=%fused_computation.10 | loop fusion | flops 4194304 | bytes 4194304 | tf_op jit(solution)/shard_map/concatenate | solution.py:57
  100.6 0.5 collective-permute-start
  101.2 0.9 divide_convert_fusion.1
  102.0 0.7 convert_element_type.97
  102.7 6.0 %multiply_convert_fusion.1 = bf16[2048,1024]{1,0:T(8,128)(2,1)S(1)} fusion(bf16[512,1024]{1,0:T(8,128)(2,1)S(1)} %convert_element_type.97, bf16[1,512,2048]{2,0,1:T(2,128)(2,1)} %pad_maximum_fusion), kind=kOutput, calls=%fused_computation.8 | convolution fusion | flops 2151677952 | bytes 7340032 | tf_op jit(solution)/shard_map/mqr,mqe->mre/dot_general | solution.py:61
  108.8 1.1 broadcast_in_dim.2
  109.8 0.6 constant_dynamic-update-slice_fusion.1
  110.5 0.0 copy-start.1
  110.5 15.9 %collective-permute-done = bf16[1,512,1024]{2,1,0:T(8,128)(2,1)} collective-permute-done((bf16[1,512,1024]{2,1,0:T(8,128)(2,1)}, bf16[1,512,1024]{2,1,0:T(8,128)(2,1)}, u32[]{:S(2)}, u32[]{:S(2)}) %collective-permute-start) | collective-permute-done | bytes 1048608 | tf_op jit(solution)/shard_map/ppermute | solution.py:11
  126.4 5.0 %multiply_convert_fusion = bf16[2048,1024]{1,0:T(8,128)(2,1)S(1)} fusion(bf16[1,512,1024]{2,1,0:T(8,128)(2,1)} %collective-permute-done, bf16[1,512,2048]{2,0,1:T(2,128)(2,1)S(1)} %copy-done.2), kind=kOutput, calls=%fused_computation.7 | convolution fusion | flops 2151677952 | bytes 7340032 | tf_op jit(solution)/shard_map/mqr,mqe->mre/dot_general | solution.py:61
  131.4 2.5 %constant_dynamic-update-slice_fusion = bf16[1,2,1024,2048]{3,2,1,0:T(8,128)(2,1)} fusion(bf16[1,2,1024,2048]{3,2,1,0:T(8,128)(2,1)} %copy-done.1, bf16[1,2,1024,1024]{3,2,1,0:T(8,128)(2,1)S(1)} %bitcast.63, s32[]{:T(128)S(6)} %select_n.33), kind=kLoop, calls=%fused_computation.57 | loop fusion | bytes 8388612 | tf_op jit(solution)/shard_map/dynamic_update_slice | solution.py:71
  (10 shorter events, 0.1 us)
Async XLA Ops:
  1.6 5.8 %copy-start = (bf16[16,1024,256]{2,1,0:T(8,128)(2,1)S(1)}, bf16[16,1024,256]{2,1,0:T(8,128)(2,1)}, u32[]{:S(2)}) copy-start(bf16[16,1024,256]{2,1,0:T(8,128)(2,1)} %param.3) | copy-start | bytes 25165828
  20.7 53.4 %all-to-all-start = ((f32[16,1,16,2,1024]{4,3,2,1,0:T(2,128)}), f32[16,1,16,2,1024]{4,3,2,1,0:T(2,128)S(1)}, u32[]{:S(2)}, u32[]{:S(2)}) async-start(f32[16,1,16,2,1024]{4,3,2,1,0:T(2,128)} %copy.23), calls=%async_computation | async-start | bytes 4194304 | tf_op jit(solution)/shard_map/all_to_all | solution.py:44
  100.6 25.8 %collective-permute-start = (bf16[1,512,1024]{2,1,0:T(8,128)(2,1)}, bf16[1,512,1024]{2,1,0:T(8,128)(2,1)}, u32[]{:S(2)}, u32[]{:S(2)}) collective-permute-start(bf16[1,512,1024]{2,1,0:T(8,128)(2,1)} %copy.27), channel_id=1, source_target_pairs={{0,1},{1,0},{2,3},{3,2},{4,5},{5,4},{6,7},{7,6},{8,9},{9,8},{10,11... | collective-permute-start | bytes 3145736 | tf_op jit(solution)/shard_map/ppermute | solution.py:11
  109.8 16.6 %copy-start.2 = (bf16[1,512,2048]{2,0,1:T(2,128)(2,1)S(1)}, bf16[1,512,2048]{2,0,1:T(2,128)(2,1)}, u32[]{:S(2)}) copy-start(bf16[1,512,2048]{2,0,1:T(2,128)(2,1)} %pad_maximum_fusion) | copy-start | bytes 6291460
  110.5 20.9 %copy-start.1 = (bf16[1,2,1024,2048]{3,2,1,0:T(8,128)(2,1)}, bf16[1,2,1024,2048]{3,2,1,0:T(8,128)(2,1)S(1)}, u32[]{:S(2)}) copy-start(bf16[1,2,1024,2048]{3,2,1,0:T(8,128)(2,1)S(1)} %constant_dynamic-update-slice_fusion.1) | copy-start | bytes 25165828
